TPU v7x, 256 devices: a whole 4x4x8 slice. The times are simulated.
256 devices in a mesh: req: 16 (over y, x_hi, core), blk: 16 (over z, x_lo).
Axes of the slice: x: 4 (x_hi: 2, x_lo: 2; x = x_hi * 2 + x_lo), y: 4, z: 8, core: 2. Of those that a mesh axis runs over, the one named last changes fastest.
Arguments:
- tokens: bfloat16 [32, 256, 1600], P('req'), may hold values from -6 to 6
- cache_kv: bfloat16 [4, 8192, 16, 128], P(None, 'req', 'blk'), may hold values from -500 to 500
- w_qkv: bfloat16 [1600, 16, 192], P(None, 'blk'), may hold values from -0.15625 to 0.15625
- w_out: bfloat16 [16, 64, 1600], P('blk'), may hold values from -0.1875 to 0.1875
- w_fc: bfloat16 [1600, 6400], P(None, 'blk'), may hold values from -0.15625 to 0.15625
- w_proj: bfloat16 [6400, 1600], P('blk'), may hold values from -0.078125 to 0.078125
- embed_table: bfloat16 [50256, 1600], P('req', 'blk'), may hold values from -6 to 6
- group_ids: int32 [32], replicated, may hold values from 0 to 3, never falling along the last dimension, each value on 1 to 16 neighbouring positions
- cache_len: int32 [4], replicated, may hold values from 512 to 8192, as said below
- accept: int32 [2, 32, 256], P(None, 'req'), may hold values 0 or 1
- new_ids: int32 [2, 32, 256], replicated, may hold values from 0 to 50255
Outputs:
- denoised: bfloat16 [32, 256, 1600], P('req')
Inputs may be any that keep to these rules, and one draw needn't show every extreme that they name: `group_ids`: requests of one group stand in consecutive order; each of the 4 groups holds 1 to 16 requests and one holds exactly 16. Cache positions 0 to cache_len[g] - 1 of group g are live; one group's cache is full in every draw.
All inputs are finite; a program needn't handle non-finite values. No bound on the sum of `accept` on one device may be relied on, other than what follows from the above.
Results may differ from a plain program's by a relative error of at most 0.04.
Values may be sent and summed in bfloat16 or wider, within the bound.
A program may use at most 128 MiB of HBM per device.

v0:
```python
import jax
import jax.numpy as jnp
from jax import lax
from jax.sharding import PartitionSpec as P

PASSES = 2


def layer_norm(values):
    centre = values - jnp.mean(values, -1, keepdims=True)
    spread = jnp.mean(centre * centre, -1, keepdims=True)
    return centre * lax.rsqrt(spread + 1e-05)


def attend(projected, own_cache, lengths, head_dim):
    queries = projected[..., :head_dim]
    keys_new = projected[..., head_dim : 2 * head_dim]
    values_new = projected[..., 2 * head_dim :]
    factor = head_dim ** (-0.5)
    scores = (
        jnp.einsum("rqhd,rkhd->rhqk", queries, keys_new, preferred_element_type=jnp.float32)
        * factor
    )
    highest = jnp.max(scores, -1)
    weights_raw = jnp.exp(scores - highest[..., None])
    totals = jnp.sum(weights_raw, -1)
    gathered = jnp.einsum(
        "rhqk,rkhd->rhqd",
        weights_raw.astype(jnp.bfloat16),
        values_new,
        preferred_element_type=jnp.float32,
    )
    cache_size = own_cache.shape[1]
    key_span = min(1024, cache_size)

    def visit_block(block_index, carried):
        highest, totals, gathered = carried
        cache_piece = lax.dynamic_slice_in_dim(own_cache, block_index * key_span, key_span, 1)
        scores = (
            jnp.einsum(
                "rqhd,rkhd->rhqk",
                queries,
                cache_piece[..., :head_dim],
                preferred_element_type=jnp.float32,
            )
            * factor
        )
        position = block_index * key_span + jnp.arange(key_span, dtype=jnp.int32)
        scores = jnp.where(
            position[None, None, None, :] < lengths[:, None, None, None], scores, -1e30
        )
        raised = jnp.maximum(highest, jnp.max(scores, -1))
        shrink = jnp.exp(highest - raised)
        weights_raw = jnp.exp(scores - raised[..., None])
        totals = totals * shrink + jnp.sum(weights_raw, -1)
        gathered = gathered * shrink[..., None] + jnp.einsum(
            "rhqk,rkhd->rhqd",
            weights_raw.astype(jnp.bfloat16),
            cache_piece[..., head_dim:],
            preferred_element_type=jnp.float32,
        )
        return (raised, totals, gathered)

    highest, totals, gathered = lax.fori_loop(
        0, cache_size // key_span, visit_block, (highest, totals, gathered)
    )
    mixed_heads = gathered / totals[..., None]
    return jnp.transpose(mixed_heads, (0, 2, 1, 3)).astype(jnp.bfloat16)


def shards(
    tokens, cache_kv, w_qkv, w_out, w_fc, w_proj, embed_table, group_ids, cache_len, accept, new_ids
):
    req_index = lax.axis_index("req")
    per_device = tokens.shape[0]
    kv_width = cache_kv.shape[3]
    head_dim = kv_width // 2
    my_groups = lax.dynamic_slice_in_dim(group_ids, req_index * per_device, per_device)
    every_cache = lax.all_gather(cache_kv, "req", axis=1, tiled=True)
    own_cache = jnp.take(every_cache, my_groups, axis=0)
    lengths = jnp.take(cache_len, my_groups)
    vocab_dev = embed_table.shape[0]
    relative = new_ids - req_index * vocab_dev
    inside = (relative >= 0) & (relative < vocab_dev)
    looked = jnp.take(embed_table, jnp.clip(relative, 0, vocab_dev - 1), axis=0)
    looked = jnp.where(inside[..., None], looked, jnp.zeros((), jnp.bfloat16))
    picked = (
        lax.psum_scatter(looked, "req", scatter_dimension=1, tiled=True)
        .astype(jnp.float32)
        .astype(jnp.bfloat16)
    )
    fresh_rows = lax.all_gather(picked, "blk", axis=3, tiled=True)
    current = tokens
    for pass_index in range(PASSES):
        state_f32 = current.astype(jnp.float32)
        normed = layer_norm(state_f32).astype(jnp.bfloat16)
        projected = jnp.einsum(
            "rbd,dhc->rbhc", normed, w_qkv, preferred_element_type=jnp.float32
        ).astype(jnp.bfloat16)
        head_rows = attend(projected, own_cache, lengths, head_dim)
        partial_terms = jnp.einsum(
            "rbhc,hcd->rbd", head_rows, w_out, preferred_element_type=jnp.float32
        )
        middle = state_f32 + lax.psum(partial_terms.astype(jnp.bfloat16), "blk").astype(jnp.float32)
        normed_mid = layer_norm(middle).astype(jnp.bfloat16)
        hidden = jax.nn.gelu(
            jnp.einsum("rbd,df->rbf", normed_mid, w_fc, preferred_element_type=jnp.float32),
            approximate=True,
        ).astype(jnp.bfloat16)
        grown_rows = jnp.einsum("rbf,fd->rbd", hidden, w_proj, preferred_element_type=jnp.float32)
        current = (
            middle + lax.psum(grown_rows.astype(jnp.bfloat16), "blk").astype(jnp.float32)
        ).astype(jnp.bfloat16)
        current = jnp.where(accept[pass_index][..., None] == 1, fresh_rows[pass_index], current)
    return current


def solution(mesh):
    return jax.shard_map(
        shards,
        mesh=mesh,
        in_specs=(
            P("req", None, None),
            P(None, "req", "blk", None),
            P(None, "blk", None),
            P("blk", None, None),
            P(None, "blk"),
            P("blk", None),
            P("req", "blk"),
            P(),
            P(),
            P(None, "req", None),
            P(),
        ),
        out_specs=P("req", None, None),
        check_vma=False,
    )
```

profile of v0, /device:TPU:6, one launch (start us, length us, event | category | flops | bytes accessed | tf_op | source)
XLA Modules:
  0.0 969.9 jit_solution(16571325852743032627)
XLA Ops:
  9.8 57.4 %gather_fusion = bf16[16384,100]{1,0:T(8,128)(2,1)} fusion(bf16[3141,100]{1,0:T(8,128)(2,1)S(1)} %copy.29, s32[16384]{0:T(1024)S(1)} %broadcast_clamp_fusion), kind=kCustom, calls=%fused_computation | custom fusion | bytes 6619136 | tf_op jit(solution)/shard_map/jit(_take)/gather | solution.py:85
  67.2 7.7 copy.44
  74.9 2.3 select_select_fusion
  77.2 5.1 copy.31
  86.8 2.7 all-gather.5.cloned.1.call-done
  89.6 5.7 slice_bitcast_fusion.1
  95.3 4.4 gather_fusion.3
  99.6 4.3 gather_fusion.2
  103.9 4.0 maximum_select_fusion
  107.9 6.4 copy.37
  114.4 34.5 %while.34 = (s32[]{:T(128)}, f32[2,1,256]{2,0,1:T(2,128)S(1)}, f32[2,1,256]{2,0,1:T(2,128)S(1)}, f32[2,1,256,64]{2,3,0,1:T(8,128)S(1)}, s32[2]{0:T(128)S(1)}, /*...) while((s32[]{:T(128)}, f32[2,1,256]{2,0,1:T(2,128)S(1)}, ...), condition=%wide.region_8.9_spmd, body=%wide.region_5.8_spmd.sunk | while | flops 140055040 | bytes 7192775 | solution.py:64
  121.1 1.8 fusion.149
  125.4 1.8 fusion.149
  129.7 1.8 fusion.149
  134.1 1.8 fusion.149
  138.4 1.8 fusion.149
  142.7 1.8 fusion.149
  147.0 1.8 fusion.149
  152.0 92.6 %all-reduce.15.cloned.1.call-done = bf16[2,32,256,100]{2,0,3,1:T(2,128)(2,1)} async-done(((bf16[2,32,256,100]{2,0,3,1:T(2,128)(2,1)}), bf16[2,32,256,100]{2,0,3,1:T(2,128)(2,1)}) %all-reduce.15.cloned.1.call-update) | async-done | bytes 3276816
  246.8 147.8 %all-reduce.7.cloned.1.call-done = bf16[2,256,1600]{1,2,0:T(8,128)(2,1)} async-done(((bf16[2,256,1600]{1,2,0:T(8,128)(2,1)}), bf16[2,256,1600]{1,2,0:T(8,128)(2,1)}) %all-reduce.7.cloned.1.call-update) | async-done | bytes 1638416 | tf_op jit(solution)/shard_map/psum | solution.py:104
  394.6 2.0 fusion.38
  397.3 5.1 convolution_convert_fusion.3
  402.5 75.9 %all-gather.3.cloned.1.call-done = bf16[2,2,256,1600]{2,1,0,3:T(2,128)(2,1)} async-done(((bf16[2,2,256,100]{2,1,0,3:T(2,128)(2,1)}), bf16[2,2,256,1600]{2,1,0,3:T(2,128)(2,1)}) %all-gather.3.cloned.1.call-update) | async-done | bytes 3276816 | tf_op jit(solution)/shard_map/all_gather | solution.py:92
  478.4 5.4 fusion.135
  483.8 139.8 %all-reduce.9.cloned.1.call-done = bf16[2,256,1600]{1,2,0:T(8,128)(2,1)} async-done(((bf16[2,256,1600]{1,2,0:T(8,128)(2,1)}), bf16[2,256,1600]{1,2,0:T(8,128)(2,1)}) %all-reduce.9.cloned.1.call-update) | async-done | bytes 1638416 | tf_op jit(solution)/shard_map/psum | solution.py:112
  623.6 3.4 convert_reduce_fusion
  628.8 34.4 %while.35 = (s32[]{:T(128)}, f32[2,1,256]{2,0,1:T(2,128)S(1)}, f32[2,1,256]{2,0,1:T(2,128)S(1)}, f32[2,1,256,64]{2,3,0,1:T(8,128)S(1)}, s32[2]{0:T(128)S(1)}, /*...) while((s32[]{:T(128)}, f32[2,1,256]{2,0,1:T(2,128)S(1)}, ...), condition=%wide.region_20.21_spmd, body=%wide.region_17.20_spmd.sunk | while | flops 140055040 | bytes 7192775 | solution.py:64
  665.4 142.6 %all-reduce.11.cloned.1.call-done = bf16[2,256,1600]{1,2,0:T(8,128)(2,1)} async-done(((bf16[2,256,1600]{1,2,0:T(8,128)(2,1)}), bf16[2,256,1600]{1,2,0:T(8,128)(2,1)}) %all-reduce.11.cloned.1.call-update) | async-done | bytes 1638416 | tf_op jit(solution)/shard_map/psum | solution.py:104
  808.0 2.0 fusion.39
  810.6 5.1 convolution_convert_fusion.2
  815.8 142.9 %all-reduce.13.cloned.1.call-done = bf16[2,256,1600]{1,2,0:T(8,128)(2,1)} async-done(((bf16[2,256,1600]{1,2,0:T(8,128)(2,1)}), bf16[2,256,1600]{1,2,0:T(8,128)(2,1)}) %all-reduce.13.cloned.1.call-update) | async-done | bytes 1638416 | tf_op jit(solution)/shard_map/psum | solution.py:112
  958.7 4.4 fusion.43
  (201 shorter events, 72.7 us)
Async XLA Ops:
  6.5 390.8 %copy-start = (bf16[400,1600]{1,0:T(8,128)(2,1)S(1)}, bf16[400,1600]{1,0:T(8,128)(2,1)}, u32[]{:S(2)}) copy-start(bf16[400,1600]{1,0:T(8,128)(2,1)} %param.20) | copy-start | bytes 3840004
  6.5 83.0 %all-gather.5.cloned.1.call-start = ((), (), s32[]{:S(2)}) async-start(), calls=%async_computation.1 | async-start | bytes 8912896 | tf_op jit(solution)/shard_map/all_gather | solution.py:79
  7.3 237.3 %all-reduce.15.cloned.1.call-start = ((), (), s32[]{:S(2)}) async-start(), calls=%async_computation.6 | async-start | bytes 6553600
  82.3 1.4 copy-start.2
  82.3 312.3 %all-reduce.7.cloned.1.call-start = ((), (), s32[]{:S(2)}) async-start(), calls=%async_computation.2 | async-start | bytes 3276800 | tf_op jit(solution)/shard_map/psum | solution.py:104
  83.7 1.1 copy-start.11
  84.8 1.3 copy-start.10
  84.8 1.4 copy-start.1
  85.5 9.8 %copy-start.7 = (bf16[2,256,1,192]{1,3,0,2:T(8,128)(2,1)}, bf16[2,256,1,192]{1,3,0,2:T(8,128)(2,1)S(1)}, u32[]{:S(2)}) copy-start(bf16[2,256,1,192]{1,3,0,2:T(8,128)(2,1)S(1)} %fusion.66) | copy-start | bytes 589828
  107.9 6.4 slice-start
  114.4 34.5 %copy-start.8 = (bf16[1,64,1600]{2,1,0:T(8,128)(2,1)S(1)}, bf16[1,64,1600]{2,1,0:T(8,128)(2,1)}, u32[]{:S(2)}) copy-start(bf16[1,64,1600]{2,1,0:T(8,128)(2,1)} %param.18) | copy-start | bytes 614404
  148.9 1.9 copy-start.13
  150.7 327.7 %all-gather.3.cloned.1.call-start = ((), (), s32[]{:S(2)}) async-start(), calls=%async_computation | async-start | bytes 3481600 | tf_op jit(solution)/shard_map/all_gather | solution.py:92
  246.6 377.0 %all-reduce.9.cloned.1.call-start = ((), (), s32[]{:S(2)}) async-start(), calls=%async_computation.3 | async-start | bytes 3276800 | tf_op jit(solution)/shard_map/psum | solution.py:112
  394.6 2.0 copy-start.5
  397.3 5.2 copy-start.9
  402.5 405.5 %all-reduce.11.cloned.1.call-start = ((), (), s32[]{:S(2)}) async-start(), calls=%async_computation.4 | async-start | bytes 3276800 | tf_op jit(solution)/shard_map/psum | solution.py:104
  623.6 3.9 copy-start.12
  627.0 1.2 copy-start.3
  663.2 144.7 %copy-start.4 = (bf16[2,256,1600]{1,2,0:T(8,128)(2,1)S(1)}, bf16[2,256,1600]{1,2,0:T(8,128)(2,1)}, u32[]{:S(2)}) copy-start(bf16[2,256,1600]{1,2,0:T(8,128)(2,1)} %copy-done.3) | copy-start | bytes 4915204
  665.1 293.6 %all-reduce.13.cloned.1.call-start = ((), (), s32[]{:S(2)}) async-start(), calls=%async_computation.5 | async-start | bytes 3276800 | tf_op jit(solution)/shard_map/psum | solution.py:112
  808.0 2.0 copy-start.6
Sparse Core Ops, SparseCore 0:
  10.1 79.3 all-gather.4
  92.2 152.3 all-reduce.14
  247.3 147.2 all-reduce.6
  396.4 81.9 all-gather.2
  481.1 142.4 all-reduce.8
  665.2 142.7 all-reduce.10
  815.9 142.7 all-reduce.12
where the time goes:
time: 971 us; the launch traced here: 970 us
  waiting for transfers between devices  745 us (77%)
  local copies, waits for them, and re-layouts  103 us (11%)
  matrix products  72.2 us (7%)
  other arithmetic  33.6 us (3%)
  between operations  14.4 us (1%)
    psum x2, waiting for transfers between devices, shards(): lax.psum(partial_terms.astype(jnp.bfloat16), 'blk').astype(jnp.float32)  290 us
    psum x2, waiting for transfers between devices, shards(): lax.psum(grown_rows.astype(jnp.bfloat16), 'blk').astype(jnp.float32)  283 us
    unnamed x8, waiting for transfers between devices  93.4 us
    all_gather x1, waiting for transfers between devices, shards(): fresh_rows = lax.all_gather(picked, 'blk', axis=3, tiled=True)  75.9 us
    gather x2, local copies, waits for them, and re-layouts, shards(): looked = jnp.take(embed_table, jnp.clip(relative, 0, vocab_dev - 1), axis=0)  65.1 us
    dot_general x16, matrix products, visit_block(): jnp.einsum('rhqk,rkhd->rhqd', weights_raw.astype(jnp.bfloat16), cache_pie...  29.2 us
    dot_general x16, matrix products, visit_block(): jnp.einsum('rqhd,rkhd->rhqk', queries, cache_piece[..., :head_dim], prefe...  26.9 us
  transfers between devices with their start and end apart: 7, of which 7 were waited for; matrix products, arithmetic and copies ran while one was open for 16% of the time, Pallas kernels for 0%

commit v1 on v0

--- a/solution.py
+++ b/solution.py
@@ -89,7 +89,8 @@
         .astype(jnp.float32)
         .astype(jnp.bfloat16)
     )
-    fresh_rows = lax.all_gather(picked, "blk", axis=3, tiled=True)
+    stack = jnp.stack([picked] * lax.axis_size("blk"))
+    fresh_rows = jnp.concatenate(lax.all_to_all(stack, "blk", 0, 0), axis=3)
     current = tokens
     for pass_index in range(PASSES):
         state_f32 = current.astype(jnp.float32)

time: 971 us -> 1050 us (1.081)
  waiting for transfers between devices: 745 us -> 813 us
    all_gather x1, waiting for transfers between devices: 2.73 us -> 97.5 us  [shards(): every_cache = lax.all_gather(cache_kv, 'req', axis=1, tiled=True)]
    all_gather x1 -> x0, waiting for transfers between devices: 75.9 us -> none  [shards(): fresh_rows = lax.all_gather(picked, 'blk', axis=3, tiled=True)]
    unnamed x8 -> x7, waiting for transfers between devices: 93.4 us -> 151 us
  transfers between devices with their start and end apart: 7 -> 7, of which waited for: 7 -> 6; matrix products, arithmetic and copies ran while one was open for 16% -> 8% of each run, Pallas kernels for 0% -> 0%
where the time goes in v1:
time: 1050 us
  waiting for transfers between devices  813 us (77%)
  local copies, waits for them, and re-layouts  103 us (10%)
  matrix products  72.2 us (7%)
  other arithmetic  38.2 us (4%)
  between operations  14.5 us (1%)
    psum x2, waiting for transfers between devices, shards(): lax.psum(partial_terms.astype(jnp.bfloat16), 'blk').astype(jnp.float32)  286 us
    psum x2, waiting for transfers between devices, shards(): lax.psum(grown_rows.astype(jnp.bfloat16), 'blk').astype(jnp.float32)  279 us
    unnamed x7, waiting for transfers between devices  151 us
    all_gather x1, waiting for transfers between devices, shards(): every_cache = lax.all_gather(cache_kv, 'req', axis=1, tiled=True)  97.5 us
    gather x2, local copies, waits for them, and re-layouts, shards(): looked = jnp.take(embed_table, jnp.clip(relative, 0, vocab_dev - 1), axis=0)  67.8 us
    dot_general x16, matrix products, visit_block(): jnp.einsum('rhqk,rkhd->rhqd', weights_raw.astype(jnp.bfloat16), cache_pie...  29.2 us
    dot_general x16, matrix products, visit_block(): jnp.einsum('rqhd,rkhd->rhqk', queries, cache_piece[..., :head_dim], prefe...  26.9 us
  transfers between devices with their start and end apart: 7, of which 6 were waited for; matrix products, arithmetic and copies ran while one was open for 8% of the time, Pallas kernels for 0%

profile of v1, /device:TPU:6, one launch (start us, length us, event | category | flops | bytes accessed | tf_op | source)
XLA Modules:
  0.0 1051.6 jit_solution(1464876640381743888)
XLA Ops:
  9.2 57.4 %gather_fusion = bf16[16384,100]{1,0:T(8,128)(2,1)} fusion(bf16[3141,100]{1,0:T(8,128)(2,1)S(1)} %copy.31, s32[16384]{0:T(1024)S(1)} %broadcast_clamp_fusion), kind=kCustom, calls=%fused_computation | custom fusion | bytes 6619136 | tf_op jit(solution)/shard_map/jit(_take)/gather | solution.py:85
  66.7 10.4 copy.32
  77.0 6.9 broadcast_select_fusion.1
  89.8 149.8 %all-reduce.15.cloned.1.call-done = bf16[2,32,256,100]{2,0,3,1:T(2,128)(2,1)} async-done(((bf16[2,32,256,100]{2,0,3,1:T(2,128)(2,1)}), bf16[2,32,256,100]{2,0,3,1:T(2,128)(2,1)}) %all-reduce.15.cloned.1.call-update) | async-done | bytes 3276816
  240.9 3.4 stack.2
  244.3 8.5 all-to-all-start
  253.0 97.5 %all-gather.2.cloned.1.call-done = bf16[4,8192,1,128]{3,1,0,2:T(8,128)(2,1)} async-done(((bf16[4,512,1,128]{3,1,0,2:T(8,128)(2,1)}), bf16[4,8192,1,128]{3,1,0,2:T(8,128)(2,1)}) %all-gather.2.cloned.1.call-update) | async-done | bytes 8388624 | tf_op jit(solution)/shard_map/all_gather | solution.py:79
  350.5 5.7 slice_bitcast_fusion.1
  356.2 4.4 gather_fusion.3
  360.5 4.3 gather_fusion.2
  364.8 4.0 maximum_select_fusion
  368.8 6.4 copy.38
  375.2 34.5 %while.34 = (s32[]{:T(128)}, f32[2,1,256]{2,0,1:T(2,128)S(1)}, f32[2,1,256]{2,0,1:T(2,128)S(1)}, f32[2,1,256,64]{2,3,0,1:T(8,128)S(1)}, s32[2]{0:T(128)S(1)}, /*...) while((s32[]{:T(128)}, f32[2,1,256]{2,0,1:T(2,128)S(1)}, ...), condition=%wide.region_8.9_spmd, body=%wide.region_5.8_spmd.sunk | while | flops 140055040 | bytes 7192775 | solution.py:64
  382.0 1.8 fusion.149
  390.6 1.8 fusion.149
  399.2 1.8 fusion.149
  407.8 1.8 fusion.149
  411.6 143.0 %all-reduce.7.cloned.1.call-done = bf16[2,256,1600]{1,2,0:T(8,128)(2,1)} async-done(((bf16[2,256,1600]{1,2,0:T(8,128)(2,1)}), bf16[2,256,1600]{1,2,0:T(8,128)(2,1)}) %all-reduce.7.cloned.1.call-update) | async-done | bytes 1638416 | tf_op jit(solution)/shard_map/psum | solution.py:105
  554.6 2.0 fusion.38
  557.3 5.1 convolution_convert_fusion.3
  562.8 5.9 fusion.135
  568.7 136.4 %all-reduce.9.cloned.1.call-done = bf16[2,256,1600]{1,2,0:T(8,128)(2,1)} async-done(((bf16[2,256,1600]{1,2,0:T(8,128)(2,1)}), bf16[2,256,1600]{1,2,0:T(8,128)(2,1)}) %all-reduce.9.cloned.1.call-update) | async-done | bytes 1638416 | tf_op jit(solution)/shard_map/psum | solution.py:113
  705.2 3.4 convert_reduce_fusion
  710.4 34.5 %while.35 = (s32[]{:T(128)}, f32[2,1,256]{2,0,1:T(2,128)S(1)}, f32[2,1,256]{2,0,1:T(2,128)S(1)}, f32[2,1,256,64]{2,3,0,1:T(8,128)S(1)}, s32[2]{0:T(128)S(1)}, /*...) while((s32[]{:T(128)}, f32[2,1,256]{2,0,1:T(2,128)S(1)}, ...), condition=%wide.region_20.21_spmd, body=%wide.region_17.20_spmd.sunk | while | flops 140055040 | bytes 7192775 | solution.py:64
  712.8 1.8 fusion.153
  721.4 1.8 fusion.153
  730.1 1.8 fusion.153
  746.7 142.9 %all-reduce.11.cloned.1.call-done = bf16[2,256,1600]{1,2,0:T(8,128)(2,1)} async-done(((bf16[2,256,1600]{1,2,0:T(8,128)(2,1)}), bf16[2,256,1600]{1,2,0:T(8,128)(2,1)}) %all-reduce.11.cloned.1.call-update) | async-done | bytes 1638416 | tf_op jit(solution)/shard_map/psum | solution.py:105
  889.6 2.0 fusion.39
  892.3 5.1 convolution_convert_fusion.2
  897.5 142.9 %all-reduce.13.cloned.1.call-done = bf16[2,256,1600]{1,2,0:T(8,128)(2,1)} async-done(((bf16[2,256,1600]{1,2,0:T(8,128)(2,1)}), bf16[2,256,1600]{1,2,0:T(8,128)(2,1)}) %all-reduce.13.cloned.1.call-update) | async-done | bytes 1638416 | tf_op jit(solution)/shard_map/psum | solution.py:113
  1040.3 4.4 fusion.43
  (202 shorter events, 71.4 us)
Async XLA Ops:
  6.5 550.8 %copy-start = (bf16[400,1600]{1,0:T(8,128)(2,1)S(1)}, bf16[400,1600]{1,0:T(8,128)(2,1)}, u32[]{:S(2)}) copy-start(bf16[400,1600]{1,0:T(8,128)(2,1)} %param.20) | copy-start | bytes 3840004
  6.5 233.1 %all-reduce.15.cloned.1.call-start = ((), (), s32[]{:S(2)}) async-start(), calls=%async_computation.6 | async-start | bytes 6553600
  83.9 1.4 copy-start.2
  83.9 266.5 %all-gather.2.cloned.1.call-start = ((), (), s32[]{:S(2)}) async-start(), calls=%async_computation.1 | async-start | bytes 8912896 | tf_op jit(solution)/shard_map/all_gather | solution.py:79
  85.3 1.1 copy-start.11
  86.0 1.0 copy-start.13
  86.0 2.4 copy-start.10
  86.1 2.5 copy-start.1
  87.1 157.2 %copy-start.7 = (bf16[2,256,1,192]{1,3,0,2:T(8,128)(2,1)}, bf16[2,256,1,192]{1,3,0,2:T(8,128)(2,1)S(1)}, u32[]{:S(2)}) copy-start(bf16[2,256,1,192]{1,3,0,2:T(8,128)(2,1)S(1)} %fusion.66) | copy-start | bytes 589828
  244.3 318.5 %all-to-all-start = ((bf16[16,2,2,256,100]{3,2,4,1,0:T(2,128)(2,1)}), bf16[16,2,2,256,100]{3,2,4,1,0:T(2,128)(2,1)}, u32[]{:S(2)}, u32[]{:S(2)}) async-start(bf16[16,2,2,256,100]{3,2,4,1,0:T(2,128)(2,1)} %stack.2), calls=%async_computation | async-start | bytes 6553600 | tf_op jit(solution)/shard_map/all_to_all | solution.py:93
  252.8 301.9 %all-reduce.7.cloned.1.call-start = ((), (), s32[]{:S(2)}) async-start(), calls=%async_computation.2 | async-start | bytes 3276800 | tf_op jit(solution)/shard_map/psum | solution.py:105
  368.8 6.4 slice-start
  375.2 34.5 %copy-start.8 = (bf16[1,64,1600]{2,1,0:T(8,128)(2,1)S(1)}, bf16[1,64,1600]{2,1,0:T(8,128)(2,1)}, u32[]{:S(2)}) copy-start(bf16[1,64,1600]{2,1,0:T(8,128)(2,1)} %param.18) | copy-start | bytes 614404
  411.5 293.6 %all-reduce.9.cloned.1.call-start = ((), (), s32[]{:S(2)}) async-start(), calls=%async_computation.3 | async-start | bytes 3276800 | tf_op jit(solution)/shard_map/psum | solution.py:113
  554.6 2.0 copy-start.5
  557.3 5.4 copy-start.9
  562.5 327.1 %all-reduce.11.cloned.1.call-start = ((), (), s32[]{:S(2)}) async-start(), calls=%async_computation.4 | async-start | bytes 3276800 | tf_op jit(solution)/shard_map/psum | solution.py:105
  705.2 3.9 copy-start.12
  708.6 1.2 copy-start.3
  744.8 144.8 %copy-start.4 = (bf16[2,256,1600]{1,2,0:T(8,128)(2,1)S(1)}, bf16[2,256,1600]{1,2,0:T(8,128)(2,1)}, u32[]{:S(2)}) copy-start(bf16[2,256,1600]{1,2,0:T(8,128)(2,1)} %copy-done.3) | copy-start | bytes 4915204
  746.7 293.6 %all-reduce.13.cloned.1.call-start = ((), (), s32[]{:S(2)}) async-start(), calls=%async_computation.5 | async-start | bytes 3276800 | tf_op jit(solution)/shard_map/psum | solution.py:113
  889.6 2.0 copy-start.6
Sparse Core Ops, SparseCore 0:
  84.0 155.5 all-reduce.14
  242.4 108.0 all-gather.1
  411.7 142.9 all-reduce.6
  562.6 142.5 all-reduce.8
  746.8 142.7 all-reduce.10
  897.6 142.6 all-reduce.12
